TPU v7x, 128 devices: a whole 4x4x4 slice. The times are simulated.
128 devices in a mesh: snap: 8 (over x, core), bond: 16 (over y, z).
Axes of the slice: x: 4, y: 4, z: 4, core: 2. Of those that a mesh axis runs over, the one named last changes fastest.
Arguments:
- yields: bfloat16 [8192, 32768], P('snap', 'bond'), may hold values from -60 to 60
- partners: int32 [256, 16], P('bond'), may hold values from -1 to 255, as said below
Outputs:
- bond_means: float32 [32768], P('bond')
- covariance_tiles: float32 [16, 256, 128, 128], P('snap', 'bond')
Inputs may be any that keep to these rules, and one draw needn't show every extreme that they name: `partners`: row i lists i first, then distinct blocks in ascending order among i + 1 to i + 56 - 1 (below 256), then -1 in the remaining slots; every row lists at least one block, and some row fills all 16 slots.
All inputs are finite; a program needn't handle non-finite values.
Results may differ from a plain program's by a relative error of at most 0.0007.
Values may be sent and summed in bfloat16 or wider, within the bound.
A program may use at most 128 MiB of HBM per device.

v0:
```python
import jax
import jax.numpy as jnp
from jax import lax
from jax.sharding import PartitionSpec as P

BLOCK = 128
REACH = 56


def from_behind(value, axis, steps):
    count = lax.axis_size(axis)
    first, last = (max(0, -steps), min(count, count - steps))
    return lax.ppermute(value, axis, [(source, source + steps) for source in range(first, last)])


def shards(yields, partners):
    snaps_local, columns = yields.shape
    blocks_local = columns // BLOCK
    total_snaps = snaps_local * lax.axis_size("snap")
    local_sums = jnp.sum(yields, axis=0, dtype=jnp.float32)
    totals = lax.psum(local_sums, "snap")
    bond_means = totals / total_snaps
    centered = (yields.astype(jnp.float32) - bond_means[None, :]).astype(jnp.bfloat16)
    extent = blocks_local + REACH - 1
    hop_count = (extent - 1) // blocks_local
    pieces = [centered]
    for distance in range(1, hop_count + 1):
        arrived = from_behind(centered, "bond", -distance)
        pieces.append(arrived)
    extended = jnp.concatenate(pieces, axis=1).reshape(snaps_local, -1, BLOCK)
    ext_blocks = extended.shape[1]
    first_block = lax.axis_index("bond") * blocks_local
    live_all = partners >= 0
    index_all = jnp.clip(jnp.where(live_all, partners - first_block, 0), 0, ext_blocks - 1)
    inverse = 1.0 / (total_snaps - 1)

    def block_tiles(args):
        block_row, index_row, live_row = args
        own_block = lax.dynamic_index_in_dim(extended, block_row, 1, keepdims=False)
        chosen = jnp.take(extended, index_row, axis=1)
        tile_sum = jnp.einsum("sa,scb->cab", own_block, chosen, preferred_element_type=jnp.float32)
        return tile_sum * (live_row.astype(jnp.float32) * inverse)[:, None, None]

    per_block = lax.map(
        block_tiles, (jnp.arange(blocks_local, dtype=jnp.int32), index_all, live_all)
    )
    covariance_tiles = lax.psum_scatter(
        jnp.transpose(per_block, (1, 0, 2, 3)), "snap", scatter_dimension=0, tiled=True
    )
    return (bond_means, covariance_tiles)


def solution(mesh):
    return jax.shard_map(
        shards,
        mesh=mesh,
        in_specs=(P("snap", "bond"), P("bond", None)),
        out_specs=(P("bond"), P("snap", "bond", None, None)),
        check_vma=False,
    )
```

profile of v0, /device:TPU:1, one launch (start us, length us, event | category | flops | bytes accessed | tf_op | source)
XLA Modules:
  0.0 981.1 jit_solution(13471164592178803008)
XLA Ops:
  7.2 6.4 copy.7
  16.4 13.4 %psum.7 = f32[2048]{0:T(1024)S(1)} all-reduce(f32[2048]{0:T(1024)S(1)} %convert_reduce_fusion), channel_id=1, replica_groups=mesh['snap'=8,'bond'=16] {'snap'}, use_global_device_ids=true, to_apply=%region_1.0 | all-reduce | flops 2048 | bytes 16384 | tf_op jit(solution)/shard_map/psum | solution.py:21
  29.9 5.2 constant_dynamic-update-slice_fusion.5
  40.4 176.5 %collective-permute-done = bf16[1024,2048]{0,1:T(8,128)(2,1)} collective-permute-done((bf16[1024,2048]{0,1:T(8,128)(2,1)}, bf16[1024,2048]{0,1:T(8,128)(2,1)}, u32[]{:S(2)}, u32[]{:S(2)}) %collective-permute-start) | collective-permute-done | bytes 4194336 | tf_op jit(solution)/shard_map/ppermute | solution.py:13
  216.9 4.6 constant_dynamic-update-slice_fusion.4
  221.5 4.6 constant_dynamic-update-slice_fusion.3
  226.1 4.7 constant_dynamic-update-slice_fusion.2
  230.7 325.9 %collective-permute-done.3 = bf16[1024,2048]{0,1:T(8,128)(2,1)} collective-permute-done((bf16[1024,2048]{0,1:T(8,128)(2,1)}, bf16[1024,2048]{0,1:T(8,128)(2,1)}, u32[]{:S(2)}, u32[]{:S(2)}) %collective-permute-start.3) | collective-permute-done | bytes 4194336 | tf_op jit(solution)/shard_map/ppermute | solution.py:13
  556.7 4.6 constant_dynamic-update-slice_fusion.1
  561.2 27.9 %copy.8 = bf16[1024,80,128]{2,0,1:T(8,128)(2,1)} copy(bf16[1024,80,128]{0,2,1:T(8,128)(2,1)} %bitcast.42) | data formatting | bytes 41943040 | tf_op jit(solution)/shard_map/while | solution.py:44
  589.1 288.5 %while.10 = (s32[]{:T(128)}, f32[16,16,128,128]{3,2,0,1:T(8,128)}, s32[16,16]{1,0:T(8,128)S(1)}, bf16[1024,80,128]{2,0,1:T(8,128)(2,1)}, s32[16]{0:T(128)S(1)}, ...) while((s32[]{:T(128)}, f32[16,16,128,128]{3,2,0,1:T(8,128)}, s32[16,16]{1,0:T(8,128)S(1)}, ...), condition=%wide.region_3.4_spmd, body=%wide.region_2.3_spmd.sunk | while | flops 539231424 | bytes 18093196 | solution.py:44
  591.8 10.0 %gather_fusion = bf16[16,1024,128]{2,1,0:T(8,128)(2,1)} fusion(bf16[1024,80,128]{2,0,1:T(8,128)(2,1)} %get-tuple-element.113, s32[1024]{0:T(1024)S(1)} %pad_clamp_fusion.2), kind=kCustom, calls=%fused_computation.clone.1 | custom fusion | bytes 8388672 | tf_op jit(solution)/shard_map/while/body/eval_jaxpr/jit(_take)/gather | solution.py:40
  601.9 3.9 fusion.28
  609.9 10.0 %gather_fusion = bf16[16,1024,128]{2,1,0:T(8,128)(2,1)} fusion(bf16[1024,80,128]{2,0,1:T(8,128)(2,1)} %get-tuple-element.113, s32[1024]{0:T(1024)S(1)} %pad_clamp_fusion.2), kind=kCustom, calls=%fused_computation.clone.1 | custom fusion | bytes 8388672 | tf_op jit(solution)/shard_map/while/body/eval_jaxpr/jit(_take)/gather | solution.py:40
  627.9 10.0 %gather_fusion = bf16[16,1024,128]{2,1,0:T(8,128)(2,1)} fusion(bf16[1024,80,128]{2,0,1:T(8,128)(2,1)} %get-tuple-element.113, s32[1024]{0:T(1024)S(1)} %pad_clamp_fusion.2), kind=kCustom, calls=%fused_computation.clone.1 | custom fusion | bytes 8388672 | tf_op jit(solution)/shard_map/while/body/eval_jaxpr/jit(_take)/gather | solution.py:40
  645.9 10.0 %gather_fusion = bf16[16,1024,128]{2,1,0:T(8,128)(2,1)} fusion(bf16[1024,80,128]{2,0,1:T(8,128)(2,1)} %get-tuple-element.113, s32[1024]{0:T(1024)S(1)} %pad_clamp_fusion.2), kind=kCustom, calls=%fused_computation.clone.1 | custom fusion | bytes 8388672 | tf_op jit(solution)/shard_map/while/body/eval_jaxpr/jit(_take)/gather | solution.py:40
  664.0 10.0 %gather_fusion = bf16[16,1024,128]{2,1,0:T(8,128)(2,1)} fusion(bf16[1024,80,128]{2,0,1:T(8,128)(2,1)} %get-tuple-element.113, s32[1024]{0:T(1024)S(1)} %pad_clamp_fusion.2), kind=kCustom, calls=%fused_computation.clone.1 | custom fusion | bytes 8388672 | tf_op jit(solution)/shard_map/while/body/eval_jaxpr/jit(_take)/gather | solution.py:40
  682.0 10.0 %gather_fusion = bf16[16,1024,128]{2,1,0:T(8,128)(2,1)} fusion(bf16[1024,80,128]{2,0,1:T(8,128)(2,1)} %get-tuple-element.113, s32[1024]{0:T(1024)S(1)} %pad_clamp_fusion.2), kind=kCustom, calls=%fused_computation.clone.1 | custom fusion | bytes 8388672 | tf_op jit(solution)/shard_map/while/body/eval_jaxpr/jit(_take)/gather | solution.py:40
  700.1 10.0 %gather_fusion = bf16[16,1024,128]{2,1,0:T(8,128)(2,1)} fusion(bf16[1024,80,128]{2,0,1:T(8,128)(2,1)} %get-tuple-element.113, s32[1024]{0:T(1024)S(1)} %pad_clamp_fusion.2), kind=kCustom, calls=%fused_computation.clone.1 | custom fusion | bytes 8388672 | tf_op jit(solution)/shard_map/while/body/eval_jaxpr/jit(_take)/gather | solution.py:40
  718.1 10.0 %gather_fusion = bf16[16,1024,128]{2,1,0:T(8,128)(2,1)} fusion(bf16[1024,80,128]{2,0,1:T(8,128)(2,1)} %get-tuple-element.113, s32[1024]{0:T(1024)S(1)} %pad_clamp_fusion.2), kind=kCustom, calls=%fused_computation.clone.1 | custom fusion | bytes 8388672 | tf_op jit(solution)/shard_map/while/body/eval_jaxpr/jit(_take)/gather | solution.py:40
  728.2 3.9 fusion.28
  736.2 10.0 %gather_fusion = bf16[16,1024,128]{2,1,0:T(8,128)(2,1)} fusion(bf16[1024,80,128]{2,0,1:T(8,128)(2,1)} %get-tuple-element.113, s32[1024]{0:T(1024)S(1)} %pad_clamp_fusion.2), kind=kCustom, calls=%fused_computation.clone.1 | custom fusion | bytes 8388672 | tf_op jit(solution)/shard_map/while/body/eval_jaxpr/jit(_take)/gather | solution.py:40
  746.2 3.9 fusion.28
  754.2 10.0 %gather_fusion = bf16[16,1024,128]{2,1,0:T(8,128)(2,1)} fusion(bf16[1024,80,128]{2,0,1:T(8,128)(2,1)} %get-tuple-element.113, s32[1024]{0:T(1024)S(1)} %pad_clamp_fusion.2), kind=kCustom, calls=%fused_computation.clone.1 | custom fusion | bytes 8388672 | tf_op jit(solution)/shard_map/while/body/eval_jaxpr/jit(_take)/gather | solution.py:40
  764.2 3.9 fusion.28
  772.2 10.0 %gather_fusion = bf16[16,1024,128]{2,1,0:T(8,128)(2,1)} fusion(bf16[1024,80,128]{2,0,1:T(8,128)(2,1)} %get-tuple-element.113, s32[1024]{0:T(1024)S(1)} %pad_clamp_fusion.2), kind=kCustom, calls=%fused_computation.clone.1 | custom fusion | bytes 8388672 | tf_op jit(solution)/shard_map/while/body/eval_jaxpr/jit(_take)/gather | solution.py:40
  790.2 10.0 %gather_fusion = bf16[16,1024,128]{2,1,0:T(8,128)(2,1)} fusion(bf16[1024,80,128]{2,0,1:T(8,128)(2,1)} %get-tuple-element.113, s32[1024]{0:T(1024)S(1)} %pad_clamp_fusion.2), kind=kCustom, calls=%fused_computation.clone.1 | custom fusion | bytes 8388672 | tf_op jit(solution)/shard_map/while/body/eval_jaxpr/jit(_take)/gather | solution.py:40
  808.2 10.0 %gather_fusion = bf16[16,1024,128]{2,1,0:T(8,128)(2,1)} fusion(bf16[1024,80,128]{2,0,1:T(8,128)(2,1)} %get-tuple-element.113, s32[1024]{0:T(1024)S(1)} %pad_clamp_fusion.2), kind=kCustom, calls=%fused_computation.clone.1 | custom fusion | bytes 8388672 | tf_op jit(solution)/shard_map/while/body/eval_jaxpr/jit(_take)/gather | solution.py:40
  826.3 10.0 %gather_fusion = bf16[16,1024,128]{2,1,0:T(8,128)(2,1)} fusion(bf16[1024,80,128]{2,0,1:T(8,128)(2,1)} %get-tuple-element.113, s32[1024]{0:T(1024)S(1)} %pad_clamp_fusion.2), kind=kCustom, calls=%fused_computation.clone.1 | custom fusion | bytes 8388672 | tf_op jit(solution)/shard_map/while/body/eval_jaxpr/jit(_take)/gather | solution.py:40
  844.3 10.0 %gather_fusion = bf16[16,1024,128]{2,1,0:T(8,128)(2,1)} fusion(bf16[1024,80,128]{2,0,1:T(8,128)(2,1)} %get-tuple-element.113, s32[1024]{0:T(1024)S(1)} %pad_clamp_fusion.2), kind=kCustom, calls=%fused_computation.clone.1 | custom fusion | bytes 8388672 | tf_op jit(solution)/shard_map/while/body/eval_jaxpr/jit(_take)/gather | solution.py:40
  862.3 10.0 %gather_fusion = bf16[16,1024,128]{2,1,0:T(8,128)(2,1)} fusion(bf16[1024,80,128]{2,0,1:T(8,128)(2,1)} %get-tuple-element.113, s32[1024]{0:T(1024)S(1)} %pad_clamp_fusion.2), kind=kCustom, calls=%fused_computation.clone.1 | custom fusion | bytes 8388672 | tf_op jit(solution)/shard_map/while/body/eval_jaxpr/jit(_take)/gather | solution.py:40
  877.7 96.6 %reduce-scatter.2.cloned.1.call-done = f32[2,16,128,128]{3,2,1,0:T(8,128)} async-done(((f32[16,16,128,128]{3,2,1,0:T(8,128)}), f32[2,16,128,128]{3,2,1,0:T(8,128)}) %reduce-scatter.2.cloned.1.call-update) | async-done | bytes 2097168 | tf_op jit(solution)/shard_map/reduce_scatter | solution.py:47
  (142 shorter events, 87.8 us)
Async XLA Ops:
  7.2 967.1 %reduce-scatter.2.cloned.1.call-start = ((), (), s32[]{:S(2)}) async-start(), calls=%async_computation.1 | async-start | bytes 18874368 | tf_op jit(solution)/shard_map/reduce_scatter | solution.py:47
  13.6 26.7 %copy-start = (s32[16,16]{1,0:T(8,128)S(1)}, s32[16,16]{1,0:T(8,128)}, u32[]{:S(2)}) copy-start(s32[16,16]{1,0:T(8,128)} %param.5) | copy-start | bytes 3076
  29.9 191.6 %copy-start.1 = (f32[2048]{0:T(1024)}, f32[2048]{0:T(1024)S(1)}, u32[]{:S(2)}) copy-start(f32[2048]{0:T(1024)S(1)} %broadcast_multiply_fusion) | copy-start | bytes 24580
  35.1 181.8 %collective-permute-start = (bf16[1024,2048]{0,1:T(8,128)(2,1)}, bf16[1024,2048]{0,1:T(8,128)(2,1)}, u32[]{:S(2)}, u32[]{:S(2)}) collective-permute-start(bf16[1024,2048]{0,1:T(8,128)(2,1)} %get-tuple-element.54), channel_id=1, source_target_pairs={{1,0},{2,1},{3,2},{4,3},{5,4},{6,5},{7,6},{8,7},{9,8},{10,9},{11,1... | collective-permute-start | bytes 12582920 | tf_op jit(solution)/shard_map/ppermute | solution.py:13
  36.4 185.1 %collective-permute-start.1 = (bf16[1024,2048]{0,1:T(8,128)(2,1)}, bf16[1024,2048]{0,1:T(8,128)(2,1)}, u32[]{:S(2)}, u32[]{:S(2)}) collective-permute-start(bf16[1024,2048]{0,1:T(8,128)(2,1)} %get-tuple-element.54), channel_id=1, source_target_pairs={{2,0},{3,1},{4,2},{5,3},{6,4},{7,5},{8,6},{9,7},{10,8},{11,9},{12,... | collective-permute-start | bytes 12582920 | tf_op jit(solution)/shard_map/ppermute | solution.py:13
  37.7 188.4 %collective-permute-start.2 = (bf16[1024,2048]{0,1:T(8,128)(2,1)}, bf16[1024,2048]{0,1:T(8,128)(2,1)}, u32[]{:S(2)}, u32[]{:S(2)}) collective-permute-start(bf16[1024,2048]{0,1:T(8,128)(2,1)} %get-tuple-element.54), channel_id=1, source_target_pairs={{3,0},{4,1},{5,2},{6,3},{7,4},{8,5},{9,6},{10,7},{11,8},{12,9},{13... | collective-permute-start | bytes 12582920 | tf_op jit(solution)/shard_map/ppermute | solution.py:13
  39.0 517.7 %collective-permute-start.3 = (bf16[1024,2048]{0,1:T(8,128)(2,1)}, bf16[1024,2048]{0,1:T(8,128)(2,1)}, u32[]{:S(2)}, u32[]{:S(2)}) collective-permute-start(bf16[1024,2048]{0,1:T(8,128)(2,1)} %get-tuple-element.54), channel_id=1, source_target_pairs={{4,0},{5,1},{6,2},{7,3},{8,4},{9,5},{10,6},{11,7},{12,8},{13,9},{1... | collective-permute-start | bytes 12582920 | tf_op jit(solution)/shard_map/ppermute | solution.py:13
Sparse Core Ops, SparseCore 0:
  877.8 96.4 reduce-scatter.1
where the time goes:
time: 983 us; the launch traced here: 981 us
  waiting for transfers between devices  599 us (61%)
  local copies, waits for them, and re-layouts  246 us (25%)
  matrix products  61.9 us (6%)
  loops' own time  33 us (3%)
  between operations  14.1 us (1%)
  blocking collectives  13.4 us (1%)
    ppermute x4, waiting for transfers between devices, from_behind(): lax.ppermute(value, axis, [(source, source + steps) for source in range(f...  502 us
    gather x16, local copies, waits for them, and re-layouts, block_tiles(): chosen = jnp.take(extended, index_row, axis=1)  160 us
    reduce_scatter x1, waiting for transfers between devices, shards(): lax.psum_scatter(jnp.transpose(per_block, (1, 0, 2, 3)), 'snap', scatter_...  96.6 us
    dot_general x16, matrix products, block_tiles(): jnp.einsum('sa,scb->cab', own_block, chosen, preferred_element_type=jnp.f...  61.9 us
    another operation x1, loops' own time, shards(): lax.map(block_tiles, (jnp.arange(blocks_local, dtype=jnp.int32), index_al...  33 us
    while x1, local copies, waits for them, and re-layouts, shards(): lax.map(block_tiles, (jnp.arange(blocks_local, dtype=jnp.int32), index_al...  27.9 us
    dynamic_update_slice x32, local copies, waits for them, and re-layouts, shards(): lax.map(block_tiles, (jnp.arange(blocks_local, dtype=jnp.int32), index_al...  22.1 us
    unnamed x8, local copies, waits for them, and re-layouts  20.3 us
  transfers between devices with their start and end apart: 5, of which 3 were waited for; matrix products, arithmetic and copies ran while one was open for 1% of the time, Pallas kernels for 0%

commit v1 on v0

v1 whole, which is shorter than its diff:
```python
import functools

import jax
import jax.numpy as jnp
from jax import lax
from jax.experimental import pallas as pl
from jax.experimental.pallas import tpu as pltpu
from jax.sharding import PartitionSpec as P

BLOCK = 128
NB = 16
SLOTS = 16
NX = 4
NZ = 4
NY = 4
PARTIAL = 7
CHUNKS = 8
LAG_A, LAG_B, LAG_C = 1, 3, 5
MESH = pl.DeviceIdType.MESH


def kernel(
    total_snaps,
    x_ref,
    partners_ref,
    mean_ref,
    out_ref,
    ext,
    own_t,
    part,
    twin,
    hop,
    last,
    sums,
    load_sem,
    mean_send,
    mean_recv,
    col_send,
    col_recv,
    twin_send,
    twin_recv,
    hop_send,
    hop_recv,
    last_send,
    last_recv,
):
    snaps = ext.shape[1]
    rows = snaps // CHUNKS
    half = CHUNKS // 2
    snap = lax.axis_index("snap")
    bond = lax.axis_index("bond")
    chip_x, core = snap // 2, lax.rem(snap, 2)
    y, z = bond // NZ, lax.rem(bond, NZ)

    def at_x(step):
        return (lax.rem(chip_x + step + NX, NX) * 2 + core, bond)

    def at_z(step):
        return (snap, y * NZ + lax.rem(z + step + NZ, NZ))

    def at_y(step):
        return (snap, lax.rem(y + step + NY, NY) * NZ + z)

    twin_id = (chip_x * 2 + 1 - core, bond)

    barrier = pltpu.get_barrier_semaphore()
    for step in range(1, 8):
        pl.semaphore_signal(
            barrier, inc=1, device_id=(lax.rem(snap + step, 8), bond), device_id_type=MESH
        )
    for device in (at_z(1), at_z(-1), at_y(1), at_y(-1)):
        pl.semaphore_signal(barrier, inc=1, device_id=device, device_id_type=MESH)

    def own_load(block):
        return pltpu.make_async_copy(
            x_ref.at[:, pl.ds(block * BLOCK, BLOCK)], ext.at[block], load_sem.at[block]
        )

    for block in range(NB):
        own_load(block).start()
    for block in range(NB):
        own_load(block).wait()
        sums[snap, pl.ds(block, 1), :] = jnp.sum(
            ext[block].astype(jnp.float32), axis=0, keepdims=True
        )
    pl.semaphore_wait(barrier, 11)

    def mean_copy(step):
        peer = lax.rem(snap + step, 8)
        return pltpu.make_async_remote_copy(
            src_ref=sums.at[snap],
            dst_ref=sums.at[snap],
            send_sem=mean_send.at[step],
            recv_sem=mean_recv.at[snap],
            device_id=(peer, bond),
            device_id_type=MESH,
        )

    def mean_arrival(step):
        peer = lax.rem(snap + step, 8)
        return pltpu.make_async_remote_copy(
            src_ref=sums.at[peer],
            dst_ref=sums.at[peer],
            send_sem=mean_send.at[step],
            recv_sem=mean_recv.at[peer],
            device_id=(peer, bond),
            device_id_type=MESH,
        )

    for step in range(1, 8):
        mean_copy(step).start()
    for step in range(1, 8):
        mean_arrival(step).wait_recv()
    for step in range(1, 8):
        mean_copy(step).wait_send()
    means = jnp.sum(sums[...], axis=0) / total_snaps
    mean_ref[...] = means

    @pl.loop(0, NB)
    def _(block):
        mean = mean_ref[pl.ds(block, 1), :]
        ext[block] = (ext[block].astype(jnp.float32) - mean).astype(jnp.bfloat16)

    def send(direction, index, source, target, count, chunk, device):
        return pltpu.make_async_remote_copy(
            src_ref=ext.at[pl.ds(source * NB, count), pl.ds(chunk * rows, rows)],
            dst_ref=ext.at[pl.ds(target * NB, count), pl.ds(chunk * rows, rows)],
            send_sem=col_send.at[direction, index],
            recv_sem=col_recv.at[target, chunk],
            device_id=device,
            device_id_type=MESH,
        )

    def arrive(target, chunk, count=NB):
        send(0, 0, target, target, count, chunk, at_z(1)).wait_recv()

    y_count = jnp.where(z == NZ - 1, PARTIAL, NB)
    second_minus = jnp.where(z == 0, 5, 2)
    second_plus = jnp.where(z == NZ - 1, 5, 2)

    def y_own(n, count):
        chunk = lax.rem(n + half, CHUNKS)
        return send(0, n, 0, 4, count, chunk, at_y(-1))

    def minus_own(n):
        chunk = lax.rem(n + half, CHUNKS)
        return send(1, n, 0, 1, NB, chunk, at_z(-1))

    def minus_forward(n):
        chunk = lax.rem(n + half, CHUNKS)
        return send(1, n, 4, 1, NB, chunk, at_z(-1))

    def minus_second(j):
        return send(1, CHUNKS + j, 1, second_minus, NB, half + j, at_z(-1))

    def plus_own(n):
        return send(2, n, 0, 3, NB, n, at_z(1))

    def plus_forward(n):
        chunk = lax.rem(n + half, CHUNKS)
        return send(2, n, 4, 3, NB, chunk, at_z(1))

    def plus_second(j):
        return send(2, CHUNKS + j, 3, second_plus, NB, j, at_z(1))

    def relay_up(j):
        return send(3, j, 5, 2, NB, j, at_y(1))

    def relay_down(j):
        return send(3, j, 5, 2, NB, half + j, at_y(-1))

    first, final = z == 0, z == NZ - 1

    @pl.loop(0, CHUNKS)
    def _(n):
        @pl.when(jnp.logical_not(final))
        def _():
            y_own(n, NB).start()

        @pl.when(jnp.logical_not(first))
        def _():
            minus_own(n).start()

        @pl.when(final)
        def _():
            plus_own(n).start()
            y_own(n, PARTIAL).start()

    @pl.loop(0, NB)
    def _(block):
        own_t[block] = jnp.transpose(ext[block])

    @pl.loop(0, half)
    def _(j):
        @pl.when(jnp.logical_not(final))
        def _():
            arrive(4, half + j)
            plus_forward(j).start()

        @pl.when(first)
        def _():
            minus_forward(j).start()
            arrive(1, half + j)
            minus_second(j).start()

        @pl.when(final)
        def _():
            arrive(1, half + j)
            minus_second(j).start()
            arrive(5, half + j)
            relay_down(j).start()
            arrive(3, j)
            plus_second(j).start()

    @pl.when(jnp.logical_not(final))
    def _():
        @pl.loop(half, CHUNKS)
        def _(n):
            arrive(4, n - half)
            plus_forward(n).start()

            @pl.when(first)
            def _():
                minus_forward(n).start()

        @pl.loop(0, half)
        def _(j):
            @pl.when(jnp.logical_not(first))
            def _():
                arrive(1, half + j)
                minus_second(j).start()

            arrive(3, j)
            plus_second(j).start()

    @pl.when(first)
    def _():
        @pl.loop(0, half)
        def _(j):
            arrive(5, j)
            relay_up(j).start()

    @pl.loop(0, half)
    def _(j):
        arrive(1, j)
        arrive(3, half + j)
        arrive(2, j)
        arrive(2, half + j)

    @pl.when(final)
    def _():
        @pl.loop(0, CHUNKS)
        def _(n):
            arrive(4, n, PARTIAL)

    owner_far = lax.rem(chip_x + 2, NX)
    owner_plus = lax.rem(chip_x + 1, NX)
    owner_minus = lax.rem(chip_x + 3, NX)
    first_block = bond * NB
    inverse = 1.0 / (total_snaps - 1)

    def twin_copy(row):
        return pltpu.make_async_remote_copy(
            src_ref=part.at[row, 1 - core],
            dst_ref=twin.at[row],
            send_sem=twin_send.at[row],
            recv_sem=twin_recv.at[row],
            device_id=twin_id,
            device_id_type=MESH,
        )

    def hop_copy(row, way):
        return pltpu.make_async_remote_copy(
            src_ref=part.at[row, core, owner_far, way],
            dst_ref=hop.at[row, way],
            send_sem=hop_send.at[row, way],
            recv_sem=hop_recv.at[row, way],
            device_id=at_x(1 - 2 * way),
            device_id_type=MESH,
        )

    def last_copy(row, way):
        return pltpu.make_async_remote_copy(
            src_ref=part.at[row, core, owner_minus if way else owner_plus],
            dst_ref=last.at[row, way],
            send_sem=last_send.at[row, way],
            recv_sem=last_recv.at[row, way],
            device_id=at_x(1 - 2 * way),
            device_id_type=MESH,
        )

    @pl.loop(0, NB + LAG_C)
    def _(t):
        @pl.when(t < NB)
        def _():
            lhs = own_t[t]
            for pair in range(SLOTS // 2):
                chosen = []
                for j in range(2):
                    partner = partners_ref[t, 2 * pair + j]
                    index = jnp.clip(partner - first_block, 0, 5 * NB - 1)
                    chosen.append(ext[index])
                tiles = jnp.dot(
                    lhs, jnp.concatenate(chosen, axis=1), preferred_element_type=jnp.float32
                )
                part[t, pair % 2, pair // 2, 0] = tiles[:, :BLOCK]
                part[t, pair % 2, pair // 2, 1] = tiles[:, BLOCK:]
            twin_copy(t).start()

        @pl.when(jnp.logical_and(t >= LAG_A, t < NB + LAG_A))
        def _():
            row = t - LAG_A
            twin_copy(row).wait_recv()
            part[row, core] += twin[row]
            hop_copy(row, 0).start()
            hop_copy(row, 1).start()

        @pl.when(jnp.logical_and(t >= LAG_B, t < NB + LAG_B))
        def _():
            row = t - LAG_B
            hop_copy(row, 0).wait_recv()
            part[row, core, owner_plus, 0] += hop[row, 0]
            last_copy(row, 0).start()
            hop_copy(row, 1).wait_recv()
            part[row, core, owner_minus, 1] += hop[row, 1]
            last_copy(row, 1).start()

        @pl.when(t >= LAG_C)
        def _():
            row = t - LAG_C
            last_copy(row, 0).wait_recv()
            last_copy(row, 1).wait_recv()
            for j in range(2):
                live = partners_ref[row, 2 * snap + j] >= 0
                scale = jnp.where(live, jnp.float32(inverse), jnp.float32(0.0))
                out_ref[j, row] = scale * (
                    part[row, core, chip_x, j] + last[row, 0, j] + last[row, 1, j]
                )

    @pl.loop(0, NB)
    def _(row):
        twin_copy(row).wait_send()
        for way in range(2):
            hop_copy(row, way).wait_send()
            last_copy(row, way).wait_send()

    @pl.loop(0, CHUNKS)
    def _(n):
        minus_own(n).wait_send()
        plus_own(n).wait_send()

        @pl.when(final)
        def _():
            y_own(n, PARTIAL).wait_send()

        @pl.when(jnp.logical_not(final))
        def _():
            y_own(n, NB).wait_send()

    @pl.loop(0, half)
    def _(j):
        minus_second(j).wait_send()
        plus_second(j).wait_send()

        @pl.when(first)
        def _():
            relay_up(j).wait_send()

        @pl.when(final)
        def _():
            relay_down(j).wait_send()


def shards(yields, partners):
    snaps, columns = yields.shape
    total_snaps = snaps * lax.axis_size("snap")
    tile = (BLOCK, BLOCK)
    f32, bf16 = jnp.float32, jnp.bfloat16
    dma = pltpu.SemaphoreType.DMA
    means, tiles = pl.pallas_call(
        functools.partial(kernel, total_snaps),
        out_shape=(
            jax.ShapeDtypeStruct((NB, BLOCK), f32),
            jax.ShapeDtypeStruct((2, NB) + tile, f32),
        ),
        in_specs=[
            pl.BlockSpec(memory_space=pl.ANY),
            pl.BlockSpec(memory_space=pltpu.SMEM),
        ],
        out_specs=(
            pl.BlockSpec(memory_space=pltpu.VMEM),
            pl.BlockSpec(memory_space=pltpu.VMEM),
        ),
        scratch_shapes=[
            pltpu.VMEM((6 * NB, snaps, BLOCK), bf16),
            pltpu.VMEM((NB, BLOCK, snaps), bf16),
            pltpu.VMEM((NB, 2, NX, 2) + tile, f32),
            pltpu.VMEM((NB, NX, 2) + tile, f32),
            pltpu.VMEM((NB, 2) + tile, f32),
            pltpu.VMEM((NB, 2, 2) + tile, f32),
            pltpu.VMEM((8, NB, BLOCK), f32),
            dma((NB,)),
            dma((8,)),
            dma((8,)),
            dma((4, CHUNKS + CHUNKS // 2)),
            dma((6, CHUNKS)),
            dma((NB,)),
            dma((NB,)),
            dma((NB, 2)),
            dma((NB, 2)),
            dma((NB, 2)),
            dma((NB, 2)),
        ],
        compiler_params=pltpu.CompilerParams(
            collective_id=0, has_side_effects=True, vmem_limit_bytes=67_000_000
        ),
    )(yields, partners)
    return means.reshape(columns), tiles


def solution(mesh):
    return jax.shard_map(
        shards,
        mesh=mesh,
        in_specs=(P("snap", "bond"), P("bond", None)),
        out_specs=(P("bond"), P("snap", "bond", None, None)),
        check_vma=False,
    )
```

time: 983 us -> 246 us (0.25)
  waiting for transfers between devices: 599 us -> 0 us
  local copies, waits for them, and re-layouts: 246 us -> 4.43 us
  Pallas kernels: 0 us -> 241 us
  matrix products: 61.9 us -> 0 us
  loops' own time: 33 us -> 0 us
  between operations: 14.1 us -> 0.64 us
  blocking collectives: 13.4 us -> 0 us
    ppermute x4 -> x0, waiting for transfers between devices: 502 us -> none  [from_behind(): lax.ppermute(value, axis, [(source, source + steps) for source in range(f...]
    pallas_call x0 -> x1, Pallas kernels: none -> 241 us  [shards(): pl.pallas_call(functools.partial(kernel, total_snaps), out_shape=(jax.Sha...]
    gather x16 -> x0, local copies, waits for them, and re-layouts: 160 us -> none  [block_tiles(): chosen = jnp.take(extended, index_row, axis=1)]
    reduce_scatter x1 -> x0, waiting for transfers between devices: 96.6 us -> none  [shards(): lax.psum_scatter(jnp.transpose(per_block, (1, 0, 2, 3)), 'snap', scatter_...]
    dot_general x16 -> x0, matrix products: 61.9 us -> none  [block_tiles(): jnp.einsum('sa,scb->cab', own_block, chosen, preferred_element_type=jnp.f...]
    another operation x1 -> x0, loops' own time: 33 us -> none  [shards(): lax.map(block_tiles, (jnp.arange(blocks_local, dtype=jnp.int32), index_al...]
    while x1 -> x0, local copies, waits for them, and re-layouts: 27.9 us -> none  [shards(): lax.map(block_tiles, (jnp.arange(blocks_local, dtype=jnp.int32), index_al...]
    dynamic_update_slice x32 -> x0, local copies, waits for them, and re-layouts: 22.1 us -> none  [shards(): lax.map(block_tiles, (jnp.arange(blocks_local, dtype=jnp.int32), index_al...]
  transfers between devices with their start and end apart: 5 -> 0, of which waited for: 3 -> 0; matrix products, arithmetic and copies ran while one was open for 1% -> 0% of each run, Pallas kernels for 0% -> 0%
where the time goes in v1:
time: 246 us
  Pallas kernels  241 us (98%)
  local copies, waits for them, and re-layouts  4.43 us (2%)
    pallas_call x1, Pallas kernels, shards(): pl.pallas_call(functools.partial(kernel, total_snaps), out_shape=(jax.Sha...  241 us

profile of v1, /device:TPU:1, one launch (start us, length us, event | category | flops | bytes accessed | tf_op | source)
XLA Modules:
  0.0 245.7 jit_solution(9565800083802656990)
XLA Ops:
  0.6 240.6 %shard_map.41 = (f32[16,128]{1,0:T(8,128)}, f32[2,16,128,128]{3,2,1,0:T(8,128)}) custom-call(bf16[1024,2048]{1,0:T(8,128)(2,1)} %x_ref.1, s32[16,16]{1,0:T(8,128)} %partners_ref.1), custom_call_target="tpu_custom_call" | custom-call | tf_op jit(solution)/shard_map/pallas_call | solution.py:380
  241.2 1.3 copy.6
  242.5 3.1 %copy.7 = f32[2,16,128,128]{3,2,1,0:T(8,128)} copy(f32[2,16,128,128]{3,2,1,0:T(8,128)} %get-tuple-element.9) | data formatting | bytes 4194304

commit v2 on v1

--- a/solution.py
+++ b/solution.py
@@ -14,7 +14,7 @@
 NZ = 4
 NY = 4
 PARTIAL = 7
-CHUNKS = 8
+CHUNKS = 16
 LAG_A, LAG_B, LAG_C = 1, 3, 5
 MESH = pl.DeviceIdType.MESH
 
@@ -32,7 +32,10 @@
     hop,
     last,
     sums,
+    means,
     load_sem,
+    sum_send,
+    sum_recv,
     mean_send,
     mean_recv,
     col_send,
@@ -61,6 +64,9 @@
     def at_y(step):
         return (snap, lax.rem(y + step + NY, NY) * NZ + z)
 
+    def at_bond(step):
+        return (snap, lax.rem(bond + step + NY * NZ, NY * NZ))
+
     twin_id = (chip_x * 2 + 1 - core, bond)
 
     barrier = pltpu.get_barrier_semaphore()
@@ -68,8 +74,11 @@
         pl.semaphore_signal(
             barrier, inc=1, device_id=(lax.rem(snap + step, 8), bond), device_id_type=MESH
         )
-    for device in (at_z(1), at_z(-1), at_y(1), at_y(-1)):
-        pl.semaphore_signal(barrier, inc=1, device_id=device, device_id_type=MESH)
+    for step in range(-4, 5):
+        if step:
+            pl.semaphore_signal(
+                barrier, inc=1, device_id=at_bond(step), device_id_type=MESH
+            )
 
     def own_load(block):
         return pltpu.make_async_copy(
@@ -80,46 +89,27 @@
         own_load(block).start()
     for block in range(NB):
         own_load(block).wait()
-        sums[snap, pl.ds(block, 1), :] = jnp.sum(
-            ext[block].astype(jnp.float32), axis=0, keepdims=True
-        )
-    pl.semaphore_wait(barrier, 11)
+    pl.semaphore_wait(barrier, 15)
+
+    def sum_copy(step, source):
+        return pltpu.make_async_remote_copy(
+            src_ref=sums.at[source],
+            dst_ref=sums.at[source],
+            send_sem=sum_send.at[step],
+            recv_sem=sum_recv.at[source],
+            device_id=(lax.rem(snap + step, 8), bond),
+            device_id_type=MESH,
+        )
 
     def mean_copy(step):
-        peer = lax.rem(snap + step, 8)
-        return pltpu.make_async_remote_copy(
-            src_ref=sums.at[snap],
-            dst_ref=sums.at[snap],
+        return pltpu.make_async_remote_copy(
+            src_ref=means.at[pl.ds(0, NB)],
+            dst_ref=means.at[pl.ds(step * NB, NB)],
             send_sem=mean_send.at[step],
-            recv_sem=mean_recv.at[snap],
-            device_id=(peer, bond),
-            device_id_type=MESH,
-        )
-
-    def mean_arrival(step):
-        peer = lax.rem(snap + step, 8)
-        return pltpu.make_async_remote_copy(
-            src_ref=sums.at[peer],
-            dst_ref=sums.at[peer],
-            send_sem=mean_send.at[step],
-            recv_sem=mean_recv.at[peer],
-            device_id=(peer, bond),
-            device_id_type=MESH,
-        )
-
-    for step in range(1, 8):
-        mean_copy(step).start()
-    for step in range(1, 8):
-        mean_arrival(step).wait_recv()
-    for step in range(1, 8):
-        mean_copy(step).wait_send()
-    means = jnp.sum(sums[...], axis=0) / total_snaps
-    mean_ref[...] = means
-
-    @pl.loop(0, NB)
-    def _(block):
-        mean = mean_ref[pl.ds(block, 1), :]
-        ext[block] = (ext[block].astype(jnp.float32) - mean).astype(jnp.bfloat16)
+            recv_sem=mean_recv.at[step],
+            device_id=at_bond(-step),
+            device_id_type=MESH,
+        )
 
     def send(direction, index, source, target, count, chunk, device):
         return pltpu.make_async_remote_copy(
@@ -186,9 +176,12 @@
             plus_own(n).start()
             y_own(n, PARTIAL).start()
 
-    @pl.loop(0, NB)
-    def _(block):
-        own_t[block] = jnp.transpose(ext[block])
+    for block in range(NB):
+        sums[snap, pl.ds(block, 1), :] = jnp.sum(
+            ext[block].astype(jnp.float32), axis=0, keepdims=True
+        )
+    for step in range(1, 8):
+        sum_copy(step, snap).start()
 
     @pl.loop(0, half)
     def _(j):
@@ -212,17 +205,37 @@
             arrive(3, j)
             plus_second(j).start()
 
+    for step in range(1, 8):
+        sum_copy(step, lax.rem(snap + step, 8)).wait_recv()
+    total = sums[0]
+    for shard in range(1, 8):
+        total += sums[shard]
+    mean_ref[...] = total / total_snaps
+    for block in range(NB):
+        means[block] = mean_ref[pl.ds(block, 1), :]
+    for step in range(1, 5):
+        mean_copy(step).start()
+
+    def centered(block):
+        return (ext[block].astype(jnp.float32) - means[block]).astype(jnp.bfloat16)
+
+    @pl.loop(half, CHUNKS)
+    def _(n):
+        @pl.when(jnp.logical_not(final))
+        def _():
+            arrive(4, n - half)
+            plus_forward(n).start()
+
+        @pl.when(first)
+        def _():
+            minus_forward(n).start()
+
+        for each in range(NB // half):
+            block = (n - half) * (NB // half) + each
+            own_t[block] = jnp.transpose(centered(block))
+
     @pl.when(jnp.logical_not(final))
     def _():
-        @pl.loop(half, CHUNKS)
-        def _(n):
-            arrive(4, n - half)
-            plus_forward(n).start()
-
-            @pl.when(first)
-            def _():
-                minus_forward(n).start()
-
         @pl.loop(0, half)
         def _(j):
             @pl.when(jnp.logical_not(first))
@@ -253,6 +266,9 @@
         def _(n):
             arrive(4, n, PARTIAL)
 
+    for step in range(1, 5):
+        mean_copy(step).wait_recv()
+
     owner_far = lax.rem(chip_x + 2, NX)
     owner_plus = lax.rem(chip_x + 1, NX)
     owner_minus = lax.rem(chip_x + 3, NX)
@@ -299,7 +315,7 @@
                 for j in range(2):
                     partner = partners_ref[t, 2 * pair + j]
                     index = jnp.clip(partner - first_block, 0, 5 * NB - 1)
-                    chosen.append(ext[index])
+                    chosen.append(centered(index))
                 tiles = jnp.dot(
                     lhs, jnp.concatenate(chosen, axis=1), preferred_element_type=jnp.float32
                 )
@@ -337,6 +353,11 @@
                     part[row, core, chip_x, j] + last[row, 0, j] + last[row, 1, j]
                 )
 
+    for step in range(1, 8):
+        sum_copy(step, snap).wait_send()
+    for step in range(1, 5):
+        mean_copy(step).wait_send()
+
     @pl.loop(0, NB)
     def _(row):
         twin_copy(row).wait_send()
@@ -377,7 +398,7 @@
     tile = (BLOCK, BLOCK)
     f32, bf16 = jnp.float32, jnp.bfloat16
     dma = pltpu.SemaphoreType.DMA
-    means, tiles = pl.pallas_call(
+    bond_means, tiles = pl.pallas_call(
         functools.partial(kernel, total_snaps),
         out_shape=(
             jax.ShapeDtypeStruct((NB, BLOCK), f32),
@@ -399,9 +420,12 @@
             pltpu.VMEM((NB, 2) + tile, f32),
             pltpu.VMEM((NB, 2, 2) + tile, f32),
             pltpu.VMEM((8, NB, BLOCK), f32),
+            pltpu.VMEM((5 * NB, 1, BLOCK), f32),
             dma((NB,)),
             dma((8,)),
             dma((8,)),
+            dma((5,)),
+            dma((5,)),
             dma((4, CHUNKS + CHUNKS // 2)),
             dma((6, CHUNKS)),
             dma((NB,)),
@@ -415,7 +439,7 @@
             collective_id=0, has_side_effects=True, vmem_limit_bytes=67_000_000
         ),
     )(yields, partners)
-    return means.reshape(columns), tiles
+    return bond_means.reshape(columns), tiles
 
 
 def solution(mesh):

time: 246 us -> 237 us (0.963)
  Pallas kernels: 241 us -> 231 us
    pallas_call x1, Pallas kernels: 241 us -> 231 us  [shards(): pl.pallas_call(functools.partial(kernel, total_snaps), out_shape=(jax.Sha...]
where the time goes in v2:
time: 237 us; the launch traced here: 236 us
  Pallas kernels  231 us (97%)
  local copies, waits for them, and re-layouts  4.43 us (2%)
    pallas_call x1, Pallas kernels, shards(): pl.pallas_call(functools.partial(kernel, total_snaps), out_shape=(jax.Sha...  231 us

profile of v2, /device:TPU:1, one launch (start us, length us, event | category | flops | bytes accessed | tf_op | source)
XLA Modules:
  0.0 236.3 jit_solution(12211251373548952700)
XLA Ops:
  0.6 231.3 %shard_map.41 = (f32[16,128]{1,0:T(8,128)}, f32[2,16,128,128]{3,2,1,0:T(8,128)}) custom-call(bf16[1024,2048]{1,0:T(8,128)(2,1)} %x_ref.1, s32[16,16]{1,0:T(8,128)} %partners_ref.1), custom_call_target="tpu_custom_call" | custom-call | tf_op jit(solution)/shard_map/pallas_call | solution.py:401
  231.9 1.3 copy.6
  233.2 3.1 %copy.7 = f32[2,16,128,128]{3,2,1,0:T(8,128)} copy(f32[2,16,128,128]{3,2,1,0:T(8,128)} %get-tuple-element.9) | data formatting | bytes 4194304

commit v3 on v2

--- a/solution.py
+++ b/solution.py
@@ -15,7 +15,13 @@
 NY = 4
 PARTIAL = 7
 CHUNKS = 16
-LAG_A, LAG_B, LAG_C = 1, 3, 5
+LOW = NB // 2
+EARLY = 5
+LATER = CHUNKS - EARLY
+DIRECT = 2
+LAG_A, LAG_B, LAG_C = 1, 2, 4
+PLUS_LAG, MINUS_LAG, RELAY_LAG = 2, 4, 5
+MEANS_AT = 2
 MESH = pl.DeviceIdType.MESH
 
 
@@ -26,6 +32,7 @@
     mean_ref,
     out_ref,
     ext,
+    late,
     own_t,
     part,
     twin,
@@ -46,10 +53,10 @@
     hop_recv,
     last_send,
     last_recv,
+    late_recv,
 ):
     snaps = ext.shape[1]
     rows = snaps // CHUNKS
-    half = CHUNKS // 2
     snap = lax.axis_index("snap")
     bond = lax.axis_index("bond")
     chip_x, core = snap // 2, lax.rem(snap, 2)
@@ -111,70 +118,175 @@
             device_id_type=MESH,
         )
 
-    def send(direction, index, source, target, count, chunk, device):
-        return pltpu.make_async_remote_copy(
-            src_ref=ext.at[pl.ds(source * NB, count), pl.ds(chunk * rows, rows)],
-            dst_ref=ext.at[pl.ds(target * NB, count), pl.ds(chunk * rows, rows)],
+    whole, lower, upper, some = (0, NB), (0, LOW), (LOW, LOW), (0, PARTIAL)
+    first, final = z == 0, z == NZ - 1
+    ahead = jnp.where(final, 0, 4)
+    behind = jnp.where(first, 4, 0)
+    second_minus = jnp.where(first, 5, 2)
+    second_plus = jnp.where(final, 5, 2)
+    UPPER_2 = 0
+
+    def upper_order(n):
+        return lax.rem(n + EARLY, CHUNKS)
+
+    def send(direction, index, source, target, blocks, chunk, device, arrival=None):
+        start, count = blocks
+        return pltpu.make_async_remote_copy(
+            src_ref=ext.at[pl.ds(source * NB + start, count), pl.ds(chunk * rows, rows)],
+            dst_ref=ext.at[pl.ds(target * NB + start, count), pl.ds(chunk * rows, rows)],
             send_sem=col_send.at[direction, index],
-            recv_sem=col_recv.at[target, chunk],
+            recv_sem=col_recv.at[target if arrival is None else arrival, chunk],
             device_id=device,
             device_id_type=MESH,
         )
 
-    def arrive(target, chunk, count=NB):
-        send(0, 0, target, target, count, chunk, at_z(1)).wait_recv()
-
-    y_count = jnp.where(z == NZ - 1, PARTIAL, NB)
-    second_minus = jnp.where(z == 0, 5, 2)
-    second_plus = jnp.where(z == NZ - 1, 5, 2)
-
-    def y_own(n, count):
-        chunk = lax.rem(n + half, CHUNKS)
-        return send(0, n, 0, 4, count, chunk, at_y(-1))
-
-    def minus_own(n):
-        chunk = lax.rem(n + half, CHUNKS)
-        return send(1, n, 0, 1, NB, chunk, at_z(-1))
-
-    def minus_forward(n):
-        chunk = lax.rem(n + half, CHUNKS)
-        return send(1, n, 4, 1, NB, chunk, at_z(-1))
-
-    def minus_second(j):
-        return send(1, CHUNKS + j, 1, second_minus, NB, half + j, at_z(-1))
-
-    def plus_own(n):
-        return send(2, n, 0, 3, NB, n, at_z(1))
-
-    def plus_forward(n):
-        chunk = lax.rem(n + half, CHUNKS)
-        return send(2, n, 4, 3, NB, chunk, at_z(1))
-
-    def plus_second(j):
-        return send(2, CHUNKS + j, 3, second_plus, NB, j, at_z(1))
-
-    def relay_up(j):
-        return send(3, j, 5, 2, NB, j, at_y(1))
-
-    def relay_down(j):
-        return send(3, j, 5, 2, NB, half + j, at_y(-1))
-
-    first, final = z == 0, z == NZ - 1
+    def arrive(target, chunk, blocks=whole, arrival=None):
+        send(0, 0, target, target, blocks, chunk, at_z(1), arrival).wait_recv()
+
+    def either(n, act):
+        @pl.when(n < EARLY)
+        def _():
+            act(whole)
+
+        @pl.when(n >= EARLY)
+        def _():
+            act(lower)
+
+    def y_own(n, blocks):
+        return send(0, n, 0, 4, blocks, n, at_y(-1))
+
+    def minus_primary(n):
+        chunk = jnp.where(first, n, upper_order(n))
+        return send(1, n, behind, 1, whole, chunk, at_z(-1))
+
+    def direct(n):
+        return send(1, n, 0, 5, whole, n, at_z(-1))
+
+    def direct_down(n):
+        return send(3, LATER + n, 5, 1, whole, n, at_y(-1))
+
+    def minus_second(n):
+        arrival = jnp.where(first, 5, UPPER_2)
+        return send(1, CHUNKS + n, 1, second_minus, upper, EARLY + n, at_z(-1), arrival)
+
+    def plus_primary(n, blocks):
+        return send(2, n, ahead, 3, blocks, n, at_z(1))
+
+    def plus_second(n, blocks):
+        return send(2, CHUNKS + n, 3, second_plus, blocks, n, at_z(1))
+
+    def relay_up(n, blocks):
+        return send(3, n, 5, 2, blocks, n, at_y(1))
+
+    def relay_down(n):
+        return send(3, n, 5, 2, upper, EARLY + n, at_y(-1), UPPER_2)
+
+    def plus_late(block):
+        return pltpu.make_async_remote_copy(
+            src_ref=ext.at[ahead * NB + LOW + block, pl.ds(EARLY * rows, LATER * rows)],
+            dst_ref=late.at[block],
+            send_sem=col_send.at[2, 2 * CHUNKS + block],
+            recv_sem=late_recv.at[block],
+            device_id=at_z(1),
+            device_id_type=MESH,
+        )
 
     @pl.loop(0, CHUNKS)
     def _(n):
         @pl.when(jnp.logical_not(final))
         def _():
-            y_own(n, NB).start()
+            y_own(n, whole).start()
 
         @pl.when(jnp.logical_not(first))
         def _():
-            minus_own(n).start()
+            minus_primary(n).start()
+
+        @pl.when(jnp.logical_and(first, n < DIRECT))
+        def _():
+            direct(n).start()
 
         @pl.when(final)
         def _():
-            plus_own(n).start()
-            y_own(n, PARTIAL).start()
+            y_own(n, some).start()
+
+            @pl.when(n < 2)
+            def _():
+                plus_primary(n, whole).start()
+
+    def centered(block):
+        return (ext[block].astype(jnp.float32) - means[block]).astype(jnp.bfloat16)
+
+    def forward(n):
+        @pl.when(jnp.logical_and(n < CHUNKS, jnp.logical_not(final)))
+        def _():
+            arrive(4, n)
+            either(n, lambda blocks: plus_primary(n, blocks).start())
+
+        @pl.when(jnp.logical_and(n < CHUNKS, first))
+        def _():
+            @pl.when(n >= DIRECT)
+            def _():
+                minus_primary(n).start()
+
+            @pl.when(n < LATER)
+            def _():
+                arrive(1, EARLY + n)
+                minus_second(n).start()
+
+        @pl.when(jnp.logical_and(n < CHUNKS - 2, final))
+        def _():
+            either(n + 2, lambda blocks: plus_primary(n + 2, blocks).start())
+
+        @pl.when(jnp.logical_and(n >= PLUS_LAG, n < CHUNKS + PLUS_LAG))
+        def _():
+            m = n - PLUS_LAG
+
+            def act(blocks):
+                arrive(3, m, blocks)
+                plus_second(m, blocks).start()
+
+            either(m, act)
+
+        middle = jnp.logical_not(jnp.logical_or(first, final))
+
+        @pl.when(jnp.logical_and(middle, jnp.logical_and(n >= MINUS_LAG, n < LATER + MINUS_LAG)))
+        def _():
+            m = n - MINUS_LAG
+            arrive(1, EARLY + m)
+            minus_second(m).start()
+
+        m_down = n - n // 3
+        m_second = m_down - EARLY
+        turn = jnp.logical_and(final, lax.rem(n, 3) != 2)
+
+        @pl.when(jnp.logical_and(final, n < DIRECT))
+        def _():
+            arrive(5, n)
+            direct_down(n).start()
+
+        @pl.when(jnp.logical_and(turn, m_down < LATER))
+        def _():
+            arrive(5, EARLY + m_down, upper)
+            relay_down(m_down).start()
+
+        @pl.when(jnp.logical_and(turn, jnp.logical_and(m_second >= 0, m_second < LATER)))
+        def _():
+            arrive(1, EARLY + m_second)
+            minus_second(m_second).start()
+
+        @pl.when(jnp.logical_and(first, jnp.logical_and(n >= RELAY_LAG, n < CHUNKS + RELAY_LAG)))
+        def _():
+            m = n - RELAY_LAG
+
+            def act(blocks):
+                arrive(5, m, blocks)
+                relay_up(m, blocks).start()
+
+            either(m, act)
+
+    @pl.loop(0, MEANS_AT)
+    def _(n):
+        forward(n)
 
     for block in range(NB):
         sums[snap, pl.ds(block, 1), :] = jnp.sum(
@@ -182,29 +294,6 @@
         )
     for step in range(1, 8):
         sum_copy(step, snap).start()
-
-    @pl.loop(0, half)
-    def _(j):
-        @pl.when(jnp.logical_not(final))
-        def _():
-            arrive(4, half + j)
-            plus_forward(j).start()
-
-        @pl.when(first)
-        def _():
-            minus_forward(j).start()
-            arrive(1, half + j)
-            minus_second(j).start()
-
-        @pl.when(final)
-        def _():
-            arrive(1, half + j)
-            minus_second(j).start()
-            arrive(5, half + j)
-            relay_down(j).start()
-            arrive(3, j)
-            plus_second(j).start()
-
     for step in range(1, 8):
         sum_copy(step, lax.rem(snap + step, 8)).wait_recv()
     total = sums[0]
@@ -216,55 +305,33 @@
     for step in range(1, 5):
         mean_copy(step).start()
 
-    def centered(block):
-        return (ext[block].astype(jnp.float32) - means[block]).astype(jnp.bfloat16)
-
-    @pl.loop(half, CHUNKS)
+    @pl.loop(MEANS_AT, CHUNKS + CHUNKS // 2)
     def _(n):
-        @pl.when(jnp.logical_not(final))
-        def _():
-            arrive(4, n - half)
-            plus_forward(n).start()
-
-        @pl.when(first)
-        def _():
-            minus_forward(n).start()
-
-        for each in range(NB // half):
-            block = (n - half) * (NB // half) + each
-            own_t[block] = jnp.transpose(centered(block))
-
-    @pl.when(jnp.logical_not(final))
-    def _():
-        @pl.loop(0, half)
-        def _(j):
-            @pl.when(jnp.logical_not(first))
-            def _():
-                arrive(1, half + j)
-                minus_second(j).start()
-
-            arrive(3, j)
-            plus_second(j).start()
-
-    @pl.when(first)
-    def _():
-        @pl.loop(0, half)
-        def _(j):
-            arrive(5, j)
-            relay_up(j).start()
-
-    @pl.loop(0, half)
-    def _(j):
-        arrive(1, j)
-        arrive(3, half + j)
-        arrive(2, j)
-        arrive(2, half + j)
+        forward(n)
+
+        @pl.when(n - MEANS_AT < NB)
+        def _():
+            own_t[n - MEANS_AT] = jnp.transpose(centered(n - MEANS_AT))
+
+    @pl.loop(0, LOW)
+    def _(block):
+        plus_late(block).start()
+
+    @pl.loop(0, EARLY)
+    def _(n):
+        arrive(2, n)
+        arrive(1, n)
+
+    @pl.loop(EARLY, CHUNKS)
+    def _(n):
+        arrive(2, n, lower)
+        arrive(2, n, upper, UPPER_2)
 
     @pl.when(final)
     def _():
         @pl.loop(0, CHUNKS)
         def _(n):
-            arrive(4, n, PARTIAL)
+            arrive(4, n, some)
 
     for step in range(1, 5):
         mean_copy(step).wait_recv()
@@ -307,6 +374,11 @@
 
     @pl.loop(0, NB + LAG_C)
     def _(t):
+        @pl.when(jnp.logical_and(t >= 1, t <= LOW))
+        def _():
+            plus_late(t - 1).wait_recv()
+            ext[3 * NB + LOW - 1 + t, pl.ds(EARLY * rows, LATER * rows)] = late[t - 1]
+
         @pl.when(t < NB)
         def _():
             lhs = own_t[t]
@@ -367,29 +439,37 @@
 
     @pl.loop(0, CHUNKS)
     def _(n):
-        minus_own(n).wait_send()
-        plus_own(n).wait_send()
+        minus_primary(n).wait_send()
+        either(n, lambda blocks: plus_primary(n, blocks).wait_send())
+        either(n, lambda blocks: plus_second(n, blocks).wait_send())
 
         @pl.when(final)
         def _():
-            y_own(n, PARTIAL).wait_send()
+            y_own(n, some).wait_send()
 
         @pl.when(jnp.logical_not(final))
         def _():
-            y_own(n, NB).wait_send()
-
-    @pl.loop(0, half)
-    def _(j):
-        minus_second(j).wait_send()
-        plus_second(j).wait_send()
+            y_own(n, whole).wait_send()
+
+        @pl.when(n < LATER)
+        def _():
+            minus_second(n).wait_send()
 
         @pl.when(first)
         def _():
-            relay_up(j).wait_send()
-
-        @pl.when(final)
-        def _():
-            relay_down(j).wait_send()
+            either(n, lambda blocks: relay_up(n, blocks).wait_send())
+
+        @pl.when(jnp.logical_and(final, n < LATER))
+        def _():
+            relay_down(n).wait_send()
+
+        @pl.when(jnp.logical_and(final, n < DIRECT))
+        def _():
+            direct_down(n).wait_send()
+
+    @pl.loop(0, LOW)
+    def _(block):
+        plus_late(block).wait_send()
 
 
 def shards(yields, partners):
@@ -414,6 +494,7 @@
         ),
         scratch_shapes=[
             pltpu.VMEM((6 * NB, snaps, BLOCK), bf16),
+            pltpu.VMEM((LOW, snaps * LATER // CHUNKS, BLOCK), bf16),
             pltpu.VMEM((NB, BLOCK, snaps), bf16),
             pltpu.VMEM((NB, 2, NX, 2) + tile, f32),
             pltpu.VMEM((NB, NX, 2) + tile, f32),
@@ -426,7 +507,7 @@
             dma((8,)),
             dma((5,)),
             dma((5,)),
-            dma((4, CHUNKS + CHUNKS // 2)),
+            dma((4, 2 * CHUNKS + LOW)),
             dma((6, CHUNKS)),
             dma((NB,)),
             dma((NB,)),
@@ -434,6 +515,7 @@
             dma((NB, 2)),
             dma((NB, 2)),
             dma((NB, 2)),
+            dma((LOW,)),
         ],
         compiler_params=pltpu.CompilerParams(
             collective_id=0, has_side_effects=True, vmem_limit_bytes=67_000_000

time: 237 us -> 223 us (0.941)
  Pallas kernels: 231 us -> 218 us
    pallas_call x1, Pallas kernels: 231 us -> 218 us  [shards(): pl.pallas_call(functools.partial(kernel, total_snaps), out_shape=(jax.Sha...]
where the time goes in v3:
time: 223 us
  Pallas kernels  218 us (98%)
  local copies, waits for them, and re-layouts  4.43 us (2%)
    pallas_call x1, Pallas kernels, shards(): pl.pallas_call(functools.partial(kernel, total_snaps), out_shape=(jax.Sha...  218 us

profile of v3, /device:TPU:1, one launch (start us, length us, event | category | flops | bytes accessed | tf_op | source)
XLA Modules:
  0.0 222.7 jit_solution(6078883132376828018)
XLA Ops:
  0.6 217.6 %shard_map.41 = (f32[16,128]{1,0:T(8,128)}, f32[2,16,128,128]{3,2,1,0:T(8,128)}) custom-call(bf16[1024,2048]{1,0:T(8,128)(2,1)} %x_ref.1, s32[16,16]{1,0:T(8,128)} %partners_ref.1), custom_call_target="tpu_custom_call" | custom-call | tf_op jit(solution)/shard_map/pallas_call | solution.py:481
  218.2 1.3 copy.6
  219.5 3.1 %copy.7 = f32[2,16,128,128]{3,2,1,0:T(8,128)} copy(f32[2,16,128,128]{3,2,1,0:T(8,128)} %get-tuple-element.9) | data formatting | bytes 4194304

commit v4 on v3

--- a/solution.py
+++ b/solution.py
@@ -481,8 +481,8 @@
     bond_means, tiles = pl.pallas_call(
         functools.partial(kernel, total_snaps),
         out_shape=(
-            jax.ShapeDtypeStruct((NB, BLOCK), f32),
-            jax.ShapeDtypeStruct((2, NB) + tile, f32),
+            pltpu.VMEM((NB, BLOCK), f32),
+            pltpu.VMEM((2, NB) + tile, f32),
         ),
         in_specs=[
             pl.BlockSpec(memory_space=pl.ANY),
@@ -518,7 +518,7 @@
             dma((LOW,)),
         ],
         compiler_params=pltpu.CompilerParams(
-            collective_id=0, has_side_effects=True, vmem_limit_bytes=67_000_000
+            collective_id=0, has_side_effects=True, vmem_limit_bytes=64_500_000
         ),
     )(yields, partners)
     return bond_means.reshape(columns), tiles

time: 223 us -> 219 us (0.982)
  local copies, waits for them, and re-layouts: 4.43 us -> 1.92 us
    unnamed x2, local copies, waits for them, and re-layouts: 4.43 us -> 1.92 us
where the time goes in v4:
time: 219 us
  Pallas kernels  216 us (99%)
    pallas_call x1, Pallas kernels, shards(): pl.pallas_call(functools.partial(kernel, total_snaps), out_shape=(pltpu.V...  216 us

profile of v4, /device:TPU:1, one launch (start us, length us, event | category | flops | bytes accessed | tf_op | source)
XLA Modules:
  0.0 218.8 jit_solution(10546793137102485892)
XLA Ops:
  0.6 216.2 %shard_map.41 = (f32[16,128]{1,0:T(8,128)S(1)}, f32[2,16,128,128]{3,2,1,0:T(8,128)S(1)}) custom-call(bf16[1024,2048]{1,0:T(8,128)(2,1)} %x_ref.1, s32[16,16]{1,0:T(8,128)} %partners_ref.1), custom_call_target="tpu_custom_call" | custom-call | tf_op jit(solution)/shard_map/pallas_call | solution.py:481
  216.9 0.6 copy.6
  217.5 1.3 copy.7

commit v5 on v4

--- a/solution.py
+++ b/solution.py
@@ -18,6 +18,8 @@
 LOW = NB // 2
 EARLY = 5
 LATER = CHUNKS - EARLY
+PUT_OFF = 4
+SIDEWAYS = 2
 DIRECT = 2
 LAG_A, LAG_B, LAG_C = 1, 2, 4
 PLUS_LAG, MINUS_LAG, RELAY_LAG = 2, 4, 5
@@ -175,6 +177,12 @@
     def plus_second(n, blocks):
         return send(2, CHUNKS + n, 3, second_plus, blocks, n, at_z(1))
 
+    def sideways(n):
+        return send(2, n, 0, 5, lower, n, at_z(1), 6)
+
+    def sideways_down(n):
+        return send(3, 2 * CHUNKS + n - (CHUNKS - SIDEWAYS), 5, 3, lower, n, at_y(-1))
+
     def relay_up(n, blocks):
         return send(3, n, 5, 2, blocks, n, at_y(1))
 
@@ -205,6 +213,10 @@
         def _():
             direct(n).start()
 
+        @pl.when(jnp.logical_and(jnp.logical_not(final), n >= CHUNKS - SIDEWAYS))
+        def _():
+            sideways(n).start()
+
         @pl.when(final)
         def _():
             y_own(n, some).start()
@@ -220,13 +232,23 @@
         @pl.when(jnp.logical_and(n < CHUNKS, jnp.logical_not(final)))
         def _():
             arrive(4, n)
-            either(n, lambda blocks: plus_primary(n, blocks).start())
+
+            @pl.when(n < CHUNKS - SIDEWAYS)
+            def _():
+                either(n, lambda blocks: plus_primary(n, blocks).start())
 
         @pl.when(jnp.logical_and(n < CHUNKS, first))
         def _():
-            @pl.when(n >= DIRECT)
+            now = jnp.logical_or(n < PUT_OFF, n >= EARLY)
+
+            @pl.when(jnp.logical_and(n >= DIRECT, now))
             def _():
                 minus_primary(n).start()
+
+            @pl.when(n == CHUNKS - 1)
+            def _():
+                for chunk in range(PUT_OFF, EARLY):
+                    minus_primary(chunk).start()
 
             @pl.when(n < LATER)
             def _():
@@ -258,6 +280,12 @@
         m_down = n - n // 3
         m_second = m_down - EARLY
         turn = jnp.logical_and(final, lax.rem(n, 3) != 2)
+
+        @pl.when(jnp.logical_and(jnp.logical_not(first), jnp.logical_and(n >= 2, n < 2 + SIDEWAYS)))
+        def _():
+            chunk = CHUNKS - SIDEWAYS + n - 2
+            arrive(5, chunk, lower, 6)
+            sideways_down(chunk).start()
 
         @pl.when(jnp.logical_and(final, n < DIRECT))
         def _():
@@ -466,6 +494,10 @@
         @pl.when(jnp.logical_and(final, n < DIRECT))
         def _():
             direct_down(n).wait_send()
+
+        @pl.when(jnp.logical_and(jnp.logical_not(first), n >= CHUNKS - SIDEWAYS))
+        def _():
+            sideways_down(n).wait_send()
 
     @pl.loop(0, LOW)
     def _(block):
@@ -508,7 +540,7 @@
             dma((5,)),
             dma((5,)),
             dma((4, 2 * CHUNKS + LOW)),
-            dma((6, CHUNKS)),
+            dma((7, CHUNKS)),
             dma((NB,)),
             dma((NB,)),
             dma((NB, 2)),

time: 219 us -> 216 us (0.986)
    pallas_call x1, Pallas kernels: 216 us -> 214 us  [shards(): pl.pallas_call(functools.partial(kernel, total_snaps), out_shape=(pltpu.V...]
where the time goes in v5:
time: 216 us
  Pallas kernels  214 us (99%)
    pallas_call x1, Pallas kernels, shards(): pl.pallas_call(functools.partial(kernel, total_snaps), out_shape=(pltpu.V...  214 us

profile of v5, /device:TPU:1, one launch (start us, length us, event | category | flops | bytes accessed | tf_op | source)
XLA Modules:
  0.0 216.1 jit_solution(10798280862045184634)
XLA Ops:
  0.6 213.6 %shard_map.41 = (f32[16,128]{1,0:T(8,128)S(1)}, f32[2,16,128,128]{3,2,1,0:T(8,128)S(1)}) custom-call(bf16[1024,2048]{1,0:T(8,128)(2,1)} %x_ref.1, s32[16,16]{1,0:T(8,128)} %partners_ref.1), custom_call_target="tpu_custom_call" | custom-call | tf_op jit(solution)/shard_map/pallas_call | solution.py:513
  214.2 0.6 copy.6
  214.8 1.3 copy.7

commit v6 on v5

--- a/solution.py
+++ b/solution.py
@@ -400,6 +400,50 @@
             device_id_type=MESH,
         )
 
+    def columns_left():
+        for step in range(1, 8):
+            sum_copy(step, snap).wait_send()
+        for step in range(1, 5):
+            mean_copy(step).wait_send()
+
+        @pl.loop(0, CHUNKS)
+        def _(n):
+            minus_primary(n).wait_send()
+            either(n, lambda blocks: plus_primary(n, blocks).wait_send())
+            either(n, lambda blocks: plus_second(n, blocks).wait_send())
+
+            @pl.when(final)
+            def _():
+                y_own(n, some).wait_send()
+
+            @pl.when(jnp.logical_not(final))
+            def _():
+                y_own(n, whole).wait_send()
+
+            @pl.when(n < LATER)
+            def _():
+                minus_second(n).wait_send()
+
+            @pl.when(first)
+            def _():
+                either(n, lambda blocks: relay_up(n, blocks).wait_send())
+
+            @pl.when(jnp.logical_and(final, n < LATER))
+            def _():
+                relay_down(n).wait_send()
+
+            @pl.when(jnp.logical_and(final, n < DIRECT))
+            def _():
+                direct_down(n).wait_send()
+
+            @pl.when(jnp.logical_and(jnp.logical_not(first), n >= CHUNKS - SIDEWAYS))
+            def _():
+                sideways_down(n).wait_send()
+
+        @pl.loop(0, LOW)
+        def _(block):
+            plus_late(block).wait_send()
+
     @pl.loop(0, NB + LAG_C)
     def _(t):
         @pl.when(jnp.logical_and(t >= 1, t <= LOW))
@@ -441,11 +485,18 @@
             part[row, core, owner_minus, 1] += hop[row, 1]
             last_copy(row, 1).start()
 
+        @pl.when(t == NB - 3)
+        def _():
+            columns_left()
+
         @pl.when(t >= LAG_C)
         def _():
             row = t - LAG_C
             last_copy(row, 0).wait_recv()
             last_copy(row, 1).wait_recv()
+            twin_copy(row).wait_send()
+            hop_copy(row, 0).wait_send()
+            hop_copy(row, 1).wait_send()
             for j in range(2):
                 live = partners_ref[row, 2 * snap + j] >= 0
                 scale = jnp.where(live, jnp.float32(inverse), jnp.float32(0.0))
@@ -453,55 +504,10 @@
                     part[row, core, chip_x, j] + last[row, 0, j] + last[row, 1, j]
                 )
 
-    for step in range(1, 8):
-        sum_copy(step, snap).wait_send()
-    for step in range(1, 5):
-        mean_copy(step).wait_send()
-
     @pl.loop(0, NB)
     def _(row):
-        twin_copy(row).wait_send()
         for way in range(2):
-            hop_copy(row, way).wait_send()
             last_copy(row, way).wait_send()
-
-    @pl.loop(0, CHUNKS)
-    def _(n):
-        minus_primary(n).wait_send()
-        either(n, lambda blocks: plus_primary(n, blocks).wait_send())
-        either(n, lambda blocks: plus_second(n, blocks).wait_send())
-
-        @pl.when(final)
-        def _():
-            y_own(n, some).wait_send()
-
-        @pl.when(jnp.logical_not(final))
-        def _():
-            y_own(n, whole).wait_send()
-
-        @pl.when(n < LATER)
-        def _():
-            minus_second(n).wait_send()
-
-        @pl.when(first)
-        def _():
-            either(n, lambda blocks: relay_up(n, blocks).wait_send())
-
-        @pl.when(jnp.logical_and(final, n < LATER))
-        def _():
-            relay_down(n).wait_send()
-
-        @pl.when(jnp.logical_and(final, n < DIRECT))
-        def _():
-            direct_down(n).wait_send()
-
-        @pl.when(jnp.logical_and(jnp.logical_not(first), n >= CHUNKS - SIDEWAYS))
-        def _():
-            sideways_down(n).wait_send()
-
-    @pl.loop(0, LOW)
-    def _(block):
-        plus_late(block).wait_send()
 
 
 def shards(yields, partners):

time: 216 us -> 216 us (level)
  no operation moved by 1% of the time
where the time goes in v6:
time: 216 us
  Pallas kernels  213 us (99%)
    pallas_call x1, Pallas kernels, shards(): pl.pallas_call(functools.partial(kernel, total_snaps), out_shape=(pltpu.V...  213 us

profile of v6, /device:TPU:1, one launch (start us, length us, event | category | flops | bytes accessed | tf_op | source)
XLA Modules:
  0.0 215.6 jit_solution(15301046283850844180)
XLA Ops:
  0.6 213.1 %shard_map.41 = (f32[16,128]{1,0:T(8,128)S(1)}, f32[2,16,128,128]{3,2,1,0:T(8,128)S(1)}) custom-call(bf16[1024,2048]{1,0:T(8,128)(2,1)} %x_ref.1, s32[16,16]{1,0:T(8,128)} %partners_ref.1), custom_call_target="tpu_custom_call" | custom-call | tf_op jit(solution)/shard_map/pallas_call | solution.py:519
  213.7 0.6 copy.6
  214.3 1.3 copy.7
